TPU v7x, 256 devices: a whole 4x4x8 slice. The times are simulated.
256 devices in a mesh: ia: 4 (over y), ja: 8 (over x, core), ka: 8 (over z).
Axes of the slice: x: 4, y: 4, z: 8, core: 2. Of those that a mesh axis runs over, the one named last changes fastest.
Arguments:
- observed: bfloat16 [4, 8, 40, 128, 32, 128], P('ia', 'ja', 'ka'), may hold values from -6 to 6
- weights: bfloat16 [4, 8, 40, 128, 32, 128], P('ia', 'ja', 'ka'), may hold values from 0 to 4, as said below
- coords: int32 [4, 8, 40, 3], P('ia', 'ja', 'ka'), may hold values from 0 to 31, as said below
- counts: int32 [4, 8, 8], P('ia', 'ja', 'ka'), may hold values from 0 to 5, as said below
- factor_rows: bfloat16 [64, 4096], P(None, ('ia', 'ja', 'ka')), may hold values from -0.75 to 0.75
- factor_cols: bfloat16 [64, 4096], P(None, ('ja', 'ka')), may hold values from -0.75 to 0.75
- factor_depth: bfloat16 [64, 1024], replicated, may hold values from -0.75 to 0.75
- core_tensor: bfloat16 [64, 64, 64], replicated, may hold values from -6 to 6
Outputs:
- rows_gradient: float32 [64, 4096], P(None, ('ia', 'ja', 'ka'))
- cols_gradient: float32 [64, 4096], P(None, ('ja', 'ka'))
- depth_gradient: float32 [64, 1024], P(None, 'ka')
- core_gradient: float32 [64, 64, 64], replicated
Inputs may be any that keep to these rules, and one draw needn't show every extreme that they name: counts[a, b, c] is the number of live slots of the device at index a of ia, b of ja, c of ka; the busiest devices hold 5. coords[a, b, c * 5 + s] = (p, q, t) with a * 8 <= p < (a + 1) * 8, b * 4 <= q < (b + 1) * 4, c * 4 <= t < (c + 1) * 4; the 5 slots of one device name distinct blocks. `weights`: zero at unobserved entries, positive at observed ones.
All inputs are finite; a program needn't handle non-finite values.
Results may differ from a plain program's by a relative error of at most 0.0012.
Values may be sent and summed in bfloat16 or wider, within the bound.
A program may use at most 64 MiB of HBM per device.

v0:
```python
import jax
import jax.numpy as jnp
from jax import lax
from jax.sharding import PartitionSpec as P

resid_scale = 1.0 / 64.0


def block_terms(observed_block, weight_block, row_factor, col_factor, depth_factor, core_tensor):
    rank_width, block_rows = row_factor.shape
    block_cols = col_factor.shape[1]
    slab_depth = depth_factor.shape[1]
    core_flat = core_tensor.reshape(rank_width * rank_width, rank_width)
    first_cube = jnp.dot(core_flat, depth_factor, preferred_element_type=jnp.float32).astype(
        jnp.bfloat16
    )
    first_cube = first_cube.reshape(rank_width, rank_width, slab_depth)
    second_cube = jnp.einsum(
        "rsk,sj->rkj", first_cube, col_factor, preferred_element_type=jnp.float32
    ).astype(jnp.bfloat16)
    second_flat = second_cube.reshape(rank_width, slab_depth * block_cols)
    model_block = lax.dot_general(
        row_factor, second_flat, (((0,), (0,)), ((), ())), preferred_element_type=jnp.float32
    )
    weight_flat = weight_block.reshape(block_rows, slab_depth * block_cols).astype(jnp.float32)
    data_flat = observed_block.reshape(block_rows, slab_depth * block_cols).astype(jnp.float32)
    residual = (weight_flat * (model_block - data_flat) * resid_scale).astype(jnp.bfloat16)
    row_term = lax.dot_general(
        second_flat, residual, (((1,), (1,)), ((), ())), preferred_element_type=jnp.float32
    )
    first_back = jnp.dot(row_factor, residual, preferred_element_type=jnp.float32).astype(
        jnp.bfloat16
    )
    back_cube = first_back.reshape(rank_width, slab_depth, block_cols)
    col_term = jnp.einsum("rsk,rkj->sj", first_cube, back_cube, preferred_element_type=jnp.float32)
    second_back = jnp.einsum(
        "sj,rkj->rsk", col_factor, back_cube, preferred_element_type=jnp.float32
    ).astype(jnp.bfloat16)
    back_flat = second_back.reshape(rank_width * rank_width, slab_depth)
    depth_term = lax.dot_general(
        core_flat, back_flat, (((0,), (0,)), ((), ())), preferred_element_type=jnp.float32
    )
    core_term = lax.dot_general(
        back_flat, depth_factor, (((1,), (1,)), ((), ())), preferred_element_type=jnp.float32
    )
    return (row_term, col_term, depth_term, core_term.reshape(rank_width, rank_width, rank_width))


def add_columns(table, piece, start_col):
    width = piece.shape[1]
    return lax.dynamic_update_slice_in_dim(
        table, lax.dynamic_slice_in_dim(table, start_col, width, 1) + piece, start_col, 1
    )


def accumulate_blocks(
    live_count,
    data_slots,
    weight_slots,
    coord_slots,
    row_table,
    col_table,
    factor_depth,
    core_tensor,
    row_base,
    col_base,
):
    rank_width = core_tensor.shape[0]
    block_rows = data_slots.shape[1]
    slab_depth = data_slots.shape[2]
    block_cols = data_slots.shape[3]
    start_sums = (
        jnp.zeros((rank_width, row_table.shape[1]), jnp.float32),
        jnp.zeros((rank_width, col_table.shape[1]), jnp.float32),
        jnp.zeros((rank_width, factor_depth.shape[1]), jnp.float32),
        jnp.zeros((rank_width, rank_width, rank_width), jnp.float32),
    )

    def add_slot(slot_index, running):
        rows_sum, cols_sum, depth_sum, core_sum = running
        position = coord_slots[slot_index]
        row_start = (position[0] - row_base) * block_rows
        col_start = (position[1] - col_base) * block_cols
        depth_start = position[2] * slab_depth
        row_factor = lax.dynamic_slice_in_dim(row_table, row_start, block_rows, 1)
        col_factor = lax.dynamic_slice_in_dim(col_table, col_start, block_cols, 1)
        depth_factor = lax.dynamic_slice_in_dim(factor_depth, depth_start, slab_depth, 1)
        block_sums = block_terms(
            data_slots[slot_index],
            weight_slots[slot_index],
            row_factor,
            col_factor,
            depth_factor,
            core_tensor,
        )
        rows_sum = add_columns(rows_sum, block_sums[0], row_start)
        cols_sum = add_columns(cols_sum, block_sums[1], col_start)
        depth_sum = add_columns(depth_sum, block_sums[2], depth_start)
        return (rows_sum, cols_sum, depth_sum, core_sum + block_sums[3])

    return lax.fori_loop(0, live_count, add_slot, start_sums)


def on_device(
    observed, weights, coords, counts, factor_rows, factor_cols, factor_depth, core_tensor
):
    slot_count = observed.shape[2]
    data_slots = observed.reshape(observed.shape[2:])
    weight_slots = weights.reshape(weights.shape[2:])
    coord_slots = coords.reshape(slot_count, 3)
    own_count = counts.reshape(())
    row_table = lax.all_gather(factor_rows, ("ja", "ka"), axis=1, tiled=True)
    col_table = lax.all_gather(factor_cols, "ka", axis=1, tiled=True)
    row_base = lax.axis_index("ia") * (row_table.shape[1] // observed.shape[3])
    col_base = lax.axis_index("ja") * (col_table.shape[1] // observed.shape[5])
    rows_sum, cols_sum, depth_sum, core_sum = accumulate_blocks(
        own_count,
        data_slots,
        weight_slots,
        coord_slots,
        row_table,
        col_table,
        factor_depth,
        core_tensor,
        row_base,
        col_base,
    )
    rows_gradient = lax.psum_scatter(rows_sum, ("ja", "ka"), scatter_dimension=1, tiled=True)
    cols_whole = lax.psum(cols_sum, "ia")
    depth_whole = lax.psum(depth_sum, ("ia", "ja"))
    cols_gradient, depth_gradient = (
        lax.psum_scatter(cols_whole, "ka", scatter_dimension=1, tiled=True),
        lax.psum_scatter(depth_whole, "ka", scatter_dimension=1, tiled=True),
    )
    core_gradient = lax.psum(core_sum, ("ia", "ja", "ka"))
    return (rows_gradient, cols_gradient, depth_gradient, core_gradient)


def solution(mesh):
    in_specs = (
        P("ia", "ja", "ka", None, None, None),
        P("ia", "ja", "ka", None, None, None),
        P("ia", "ja", "ka", None),
        P("ia", "ja", "ka"),
        P(None, ("ia", "ja", "ka")),
        P(None, ("ja", "ka")),
        P(),
        P(),
    )
    out_specs = (P(None, ("ia", "ja", "ka")), P(None, ("ja", "ka")), P(None, "ka"), P())
    return jax.shard_map(
        on_device, mesh=mesh, in_specs=in_specs, out_specs=out_specs, check_vma=False
    )
```

profile of v0, /device:TPU:2, one launch (start us, length us, event | category | flops | bytes accessed | tf_op | source)
XLA Modules:
  0.0 616.1 jit_solution(5447334796632463020)
XLA Ops:
  8.0 46.2 %all_gather.7 = bf16[64,1024]{0,1:T(8,128)(2,1)S(1)} all-gather(bf16[64,16]{0,1:T(8,128)(2,1)} %param.14), channel_id=1, replica_groups=mesh['ia'=4,'ja'=8,'ka'=8] {'ja','ka'}, dimensions={1}, use_global_device_ids=true | all-gather | bytes 133120 | tf_op jit(solution)/shard_map/all_gather | solution.py:112
  54.3 1.1 copy.25
  55.5 0.8 copy.23
  56.3 24.6 %all_gather.6 = bf16[64,512]{0,1:T(8,128)(2,1)S(1)} all-gather(bf16[64,64]{0,1:T(8,128)(2,1)S(1)} %copy.23), channel_id=1, replica_groups=mesh['ia'=4,'ja'=8,'ka'=8] {'ka'}, dimensions={1}, use_global_device_ids=true | all-gather | bytes 73728 | tf_op jit(solution)/shard_map/all_gather | solution.py:113
  81.0 0.7 copy.56
  81.7 1.6 broadcast_in_dim.7
  83.3 70.1 %while.16 = (s32[]{:T(128)}, f32[64,1024]{1,0:T(8,128)S(1)}, f32[64,512]{1,0:T(8,128)S(1)}, f32[64,1024]{0,1:T(8,128)S(1)}, f32[64,64,64]{2,1,0:T(8,128)}, /*ind...) while((s32[]{:T(128)}, f32[64,1024]{1,0:T(8,128)S(1)}, ...), condition=%wide.region_1.0_spmd, body=%wide.region_0.0_spmd.sunk | while | flops 356534272 | bytes 34849308 | solution.py:101
  84.1 0.6 fusion.87
  85.3 0.4 fusion.88
  85.7 0.6 reshape.62
  88.0 2.1 dynamic-slice_convert_fusion.3
  90.1 2.7 fusion.89
  93.5 0.9 copy-done.1
  94.4 0.7 convolution_add_fusion.3
  95.4 1.0 copy-done.2
  96.7 0.5 fusion.90
  98.0 0.6 fusion.87
  99.2 0.4 fusion.88
  99.6 0.6 reshape.62
  101.9 2.1 dynamic-slice_convert_fusion.3
  104.0 2.7 fusion.89
  107.4 0.9 copy-done.1
  108.3 0.7 convolution_add_fusion.3
  109.3 1.0 copy-done.2
  110.6 0.5 fusion.90
  111.8 0.6 fusion.87
  113.0 0.4 fusion.88
  113.5 0.6 reshape.62
  115.7 2.1 dynamic-slice_convert_fusion.3
  117.9 2.7 fusion.89
  121.3 0.9 copy-done.1
  122.2 0.7 convolution_add_fusion.3
  123.2 1.0 copy-done.2
  124.5 0.5 fusion.90
  125.7 0.6 fusion.87
  126.9 0.4 fusion.88
  127.4 0.6 reshape.62
  129.6 2.1 dynamic-slice_convert_fusion.3
  131.8 2.7 fusion.89
  135.2 0.9 copy-done.1
  136.0 0.7 convolution_add_fusion.3
  137.1 1.0 copy-done.2
  138.3 0.5 fusion.90
  139.6 0.6 fusion.87
  140.8 0.4 fusion.88
  141.2 0.6 reshape.62
  143.5 2.1 dynamic-slice_convert_fusion.3
  145.6 2.7 fusion.89
  149.0 0.9 copy-done.1
  149.9 0.7 convolution_add_fusion.3
  150.9 1.0 copy-done.2
  152.2 0.5 fusion.90
  153.4 1.0 copy.28
  154.5 0.8 copy.31
  155.4 0.9 copy.29
  156.4 0.7 all-reduce.4.cloned.1.call-update
  157.1 0.6 dynamic-slice
  158.3 179.5 %all-reduce.6.cloned.1.call-done = f32[64,1024]{0,1:T(8,128)} async-done(((f32[64,1024]{0,1:T(8,128)}), f32[64,1024]{0,1:T(8,128)}) %all-reduce.6.cloned.1.call-update) | async-done | bytes 262160
  337.8 1.3 constant_dynamic-slice_fusion.1
  339.1 0.8 copy.32
  340.0 17.6 %psum.24 = f32[64,64]{1,0:T(8,128)} all-reduce(f32[64,64]{1,0:T(8,128)S(1)} %copy.32), channel_id=1, replica_groups=mesh['ia'=4,'ja'=8,'ka'=8] {'ia'}, use_global_device_ids=true, to_apply=%region_3.0 | all-reduce | flops 4096 | bytes 32768 | tf_op jit(solution)/shard_map/psum | solution.py:129
  357.6 119.0 %psum.25 = f32[64,128]{1,0:T(8,128)} all-reduce(f32[64,128]{1,0:T(8,128)} %reduce-scatter.5.cloned.1.call-done), channel_id=1, replica_groups=mesh['ia'=4,'ja'=8,'ka'=8] {'ia','ja'}, use_global_device_ids=true, to_apply=%region_5.0 | all-reduce | flops 8192 | bytes 65536 | tf_op jit(solution)/shard_map/psum | solution.py:130
  476.6 129.0 %all-reduce.4.cloned.1.call-done = f32[64,64,64]{2,1,0:T(8,128)} async-done(((f32[64,64,64]{2,1,0:T(8,128)}), f32[64,64,64]{2,1,0:T(8,128)}) %all-reduce.4.cloned.1.call-update) | async-done | bytes 1048592 | tf_op jit(solution)/shard_map/psum | solution.py:135
  605.5 3.2 copy.91
  (63 shorter events, 9.4 us)
Async XLA Ops:
  8.0 329.8 %all-reduce.6.cloned.1.call-start = ((), (), s32[]{:S(2)}) async-start(), calls=%async_computation.5 | async-start | bytes 1048576
  54.2 29.1 %copy-start = (bf16[64,64,64]{2,1,0:T(8,128)(2,1)S(1)}, bf16[64,64,64]{2,1,0:T(8,128)(2,1)}, u32[]{:S(2)}) copy-start(bf16[64,64,64]{2,1,0:T(8,128)(2,1)} %param.17) | copy-start | bytes 1572868
  92.8 1.6 copy-start.1
  95.1 1.3 copy-start.2
  106.7 1.6 copy-start.1
  109.0 1.3 copy-start.2
  120.6 1.6 copy-start.1
  122.8 1.3 copy-start.2
  134.4 1.6 copy-start.1
  136.7 1.3 copy-start.2
  148.3 1.6 copy-start.1
  150.6 1.3 copy-start.2
  154.4 2.7 copy-start.3
  154.4 184.7 %reduce-scatter.7.cloned.1.call-start = ((), (), s32[]{:S(2)}) async-start(), calls=%async_computation.4 | async-start | bytes 294912
  155.3 202.3 %reduce-scatter.5.cloned.1.call-start = ((), (), s32[]{:S(2)}) async-start(), calls=%async_computation.3 | async-start | bytes 294912 | tf_op jit(solution)/shard_map/reduce_scatter | solution.py:133
  156.3 449.2 %all-reduce.4.cloned.1.call-start = ((), (), s32[]{:S(2)}) async-start(), calls=%async_computation.2 | async-start | bytes 4194304 | tf_op jit(solution)/shard_map/psum | solution.py:135
Sparse Core Ops, SparseCore 0:
  154.6 183.2 all-reduce.5
  343.8 261.6 all-reduce.3
Sparse Core Ops, SparseCore 1:
  157.4 36.2 reduce-scatter.6
  196.0 35.9 reduce-scatter.4
where the time goes:
time: 617 us; the launch traced here: 616 us
  waiting for transfers between devices  309 us (50%)
  blocking collectives  207 us (34%)
  matrix products  29.4 us (5%)
  local copies, waits for them, and re-layouts  29.1 us (5%)
  between operations  16.2 us (3%)
  loops' own time  14 us (2%)
  other arithmetic  10.7 us (2%)
    unnamed x6, waiting for transfers between devices  180 us
    psum x1, waiting for transfers between devices, on_device(): core_gradient = lax.psum(core_sum, ('ia', 'ja', 'ka'))  129 us
    psum x1, blocking collectives, on_device(): depth_whole = lax.psum(depth_sum, ('ia', 'ja'))  119 us
    all_gather x1, blocking collectives, on_device(): row_table = lax.all_gather(factor_rows, ('ja', 'ka'), axis=1, tiled=True)  46.2 us
    all_gather x1, blocking collectives, on_device(): col_table = lax.all_gather(factor_cols, 'ka', axis=1, tiled=True)  24.6 us
    psum x1, blocking collectives, on_device(): cols_whole = lax.psum(cols_sum, 'ia')  17.6 us
    another operation x1, loops' own time, accumulate_blocks(): return lax.fori_loop(0, live_count, add_slot, start_sums)  14 us
    dot_general x5, matrix products, block_terms(): lax.dot_general(row_factor, second_flat, (((0,), (0,)), ((), ())), prefer...  13.4 us
  transfers between devices with their start and end apart: 4, of which 2 were waited for; matrix products, arithmetic and copies ran while one was open for 1% of the time, Pallas kernels for 0%

commit v1 on v0

--- a/solution.py
+++ b/solution.py
@@ -132,7 +132,8 @@
         lax.psum_scatter(cols_whole, "ka", scatter_dimension=1, tiled=True),
         lax.psum_scatter(depth_whole, "ka", scatter_dimension=1, tiled=True),
     )
-    core_gradient = lax.psum(core_sum, ("ia", "ja", "ka"))
+    half = lax.psum(core_sum, "ia")
+    core_gradient = lax.psum(half, ("ja", "ka"))
     return (rows_gradient, cols_gradient, depth_gradient, core_gradient)
 
 

time: 617 us -> 425 us (0.69)
  waiting for transfers between devices: 309 us -> 120 us
    unnamed x6, waiting for transfers between devices: 180 us -> 59.6 us
    psum x1, waiting for transfers between devices: 129 us -> 59.9 us  [on_device(): half = lax.psum(core_sum, 'ia')]
where the time goes in v1:
time: 425 us; the launch traced here: 424 us
  blocking collectives  205 us (48%)
  waiting for transfers between devices  120 us (28%)
  matrix products  29.5 us (7%)
  local copies, waits for them, and re-layouts  28.8 us (7%)
  between operations  16.2 us (4%)
  loops' own time  13.6 us (3%)
  other arithmetic  10.7 us (3%)
    psum x1, blocking collectives, on_device(): depth_whole = lax.psum(depth_sum, ('ia', 'ja'))  119 us
    psum x1, waiting for transfers between devices, on_device(): half = lax.psum(core_sum, 'ia')  59.9 us
    unnamed x6, waiting for transfers between devices  59.6 us
    all_gather x1, blocking collectives, on_device(): row_table = lax.all_gather(factor_rows, ('ja', 'ka'), axis=1, tiled=True)  46.2 us
    all_gather x1, blocking collectives, on_device(): col_table = lax.all_gather(factor_cols, 'ka', axis=1, tiled=True)  24.6 us
    psum x1, blocking collectives, on_device(): cols_whole = lax.psum(cols_sum, 'ia')  15.7 us
    another operation x1, loops' own time, accumulate_blocks(): return lax.fori_loop(0, live_count, add_slot, start_sums)  13.6 us
    dot_general x5, matrix products, block_terms(): lax.dot_general(row_factor, second_flat, (((0,), (0,)), ((), ())), prefer...  13.3 us
  transfers between devices with their start and end apart: 4, of which 2 were waited for; matrix products, arithmetic and copies ran while one was open for 1% of the time, Pallas kernels for 0%

profile of v1, /device:TPU:2, one launch (start us, length us, event | category | flops | bytes accessed | tf_op | source)
XLA Modules:
  0.0 423.7 jit_solution(11345090355918809414)
XLA Ops:
  8.0 46.2 %all_gather.7 = bf16[64,1024]{0,1:T(8,128)(2,1)S(1)} all-gather(bf16[64,16]{0,1:T(8,128)(2,1)} %param.14), channel_id=1, replica_groups=mesh['ia'=4,'ja'=8,'ka'=8] {'ja','ka'}, dimensions={1}, use_global_device_ids=true | all-gather | bytes 133120 | tf_op jit(solution)/shard_map/all_gather | solution.py:112
  54.3 1.1 copy.25
  55.5 0.8 copy.23
  56.3 24.6 %all_gather.6 = bf16[64,512]{0,1:T(8,128)(2,1)S(1)} all-gather(bf16[64,64]{0,1:T(8,128)(2,1)S(1)} %copy.23), channel_id=1, replica_groups=mesh['ia'=4,'ja'=8,'ka'=8] {'ka'}, dimensions={1}, use_global_device_ids=true | all-gather | bytes 73728 | tf_op jit(solution)/shard_map/all_gather | solution.py:113
  81.0 0.7 copy.56
  81.7 1.6 broadcast_in_dim.7
  83.3 69.4 %while.16 = (s32[]{:T(128)}, f32[64,1024]{1,0:T(8,128)S(1)}, f32[64,512]{1,0:T(8,128)S(1)}, f32[64,1024]{0,1:T(8,128)S(1)}, f32[64,64,64]{2,1,0:T(8,128)}, /*ind...) while((s32[]{:T(128)}, f32[64,1024]{1,0:T(8,128)S(1)}, ...), condition=%wide.region_1.0_spmd, body=%wide.region_0.0_spmd.sunk | while | flops 356534272 | bytes 34849308 | solution.py:101
  84.1 0.6 fusion.87
  85.2 0.4 fusion.88
  85.6 0.6 reshape.62
  86.8 0.4 convolution_convert_fusion.6
  87.9 2.1 dynamic-slice_convert_fusion.3
  90.0 2.7 fusion.89
  93.4 0.9 copy-done.1
  94.3 0.7 convolution_add_fusion.3
  95.3 1.0 copy-done.2
  96.6 0.5 fusion.90
  97.8 0.6 fusion.87
  98.9 0.4 fusion.88
  99.4 0.6 reshape.62
  101.6 2.1 dynamic-slice_convert_fusion.3
  103.8 2.7 fusion.89
  107.1 0.9 copy-done.1
  108.0 0.7 convolution_add_fusion.3
  109.0 1.0 copy-done.2
  110.3 0.5 fusion.90
  111.6 0.6 fusion.87
  112.7 0.4 fusion.88
  113.1 0.6 reshape.62
  115.4 2.1 dynamic-slice_convert_fusion.3
  117.5 2.7 fusion.89
  120.9 0.9 copy-done.1
  121.8 0.7 convolution_add_fusion.3
  122.8 1.0 copy-done.2
  124.1 0.5 fusion.90
  125.3 0.6 fusion.87
  126.4 0.4 fusion.88
  126.9 0.6 reshape.62
  129.1 2.1 dynamic-slice_convert_fusion.3
  131.3 2.7 fusion.89
  134.7 0.9 copy-done.1
  135.5 0.7 convolution_add_fusion.3
  136.6 1.0 copy-done.2
  137.8 0.5 fusion.90
  139.1 0.6 fusion.87
  140.2 0.4 fusion.88
  140.6 0.6 reshape.62
  142.9 2.1 dynamic-slice_convert_fusion.3
  145.0 2.7 fusion.89
  148.4 0.9 copy-done.1
  149.3 0.7 convolution_add_fusion.3
  150.3 1.0 copy-done.2
  151.6 0.5 fusion.90
  152.8 0.8 copy.31
  153.7 0.9 copy.29
  154.7 1.0 copy.28
  155.7 59.9 %all-reduce.5.cloned.1.call-done = f32[64,64,64]{2,1,0:T(8,128)} async-done(((f32[64,64,64]{2,1,0:T(8,128)}), f32[64,64,64]{2,1,0:T(8,128)}) %all-reduce.5.cloned.1.call-update) | async-done | bytes 1048592 | tf_op jit(solution)/shard_map/psum | solution.py:135
  215.7 0.6 dynamic-slice
  217.0 0.8 copy.32
  217.8 15.7 %psum.32 = f32[64,64]{1,0:T(8,128)} all-reduce(f32[64,64]{1,0:T(8,128)S(1)} %copy.32), channel_id=1, replica_groups=mesh['ia'=4,'ja'=8,'ka'=8] {'ia'}, use_global_device_ids=true, to_apply=%region_3.0 | all-reduce | flops 4096 | bytes 32768 | tf_op jit(solution)/shard_map/psum | solution.py:129
  233.5 118.7 %psum.33 = f32[64,128]{1,0:T(8,128)} all-reduce(f32[64,128]{1,0:T(8,128)} %reduce-scatter.5.cloned.1.call-done), channel_id=1, replica_groups=mesh['ia'=4,'ja'=8,'ka'=8] {'ia','ja'}, use_global_device_ids=true, to_apply=%region_5.0 | all-reduce | flops 8192 | bytes 65536 | tf_op jit(solution)/shard_map/psum | solution.py:130
  352.3 59.5 %all-reduce.7.cloned.1.call-done = (f32[64,1024]{0,1:T(8,128)}, f32[64,64,64]{2,1,0:T(8,128)}) async-done(((f32[64,1024]{0,1:T(8,128)}, f32[64,64,64]{2,1,0:T(8,128)}), (f32[64,1024]{0,1:T(8,128)}, f32[64,64,64]{2,1,0:T(8,128)})) %all-reduce.7.cloned.1.call-update) | async-done | bytes 1310736
  411.8 1.3 constant_dynamic-slice_fusion.1
  413.1 3.2 copy.92
  (63 shorter events, 9.2 us)
Async XLA Ops:
  8.0 207.7 %all-reduce.5.cloned.1.call-start = ((), (), s32[]{:S(2)}) async-start(), calls=%async_computation.2 | async-start | bytes 4194304 | tf_op jit(solution)/shard_map/psum | solution.py:135
  54.2 29.1 %copy-start = (bf16[64,64,64]{2,1,0:T(8,128)(2,1)S(1)}, bf16[64,64,64]{2,1,0:T(8,128)(2,1)}, u32[]{:S(2)}) copy-start(bf16[64,64,64]{2,1,0:T(8,128)(2,1)} %param.17) | copy-start | bytes 1572868
  92.7 1.6 copy-start.1
  94.9 1.3 copy-start.2
  106.4 1.6 copy-start.1
  108.7 1.3 copy-start.2
  120.2 1.6 copy-start.1
  122.4 1.3 copy-start.2
  133.9 1.6 copy-start.1
  136.2 1.3 copy-start.2
  147.7 1.6 copy-start.1
  150.0 1.3 copy-start.2
  152.8 64.2 %reduce-scatter.7.cloned.1.call-start = ((), (), s32[]{:S(2)}) async-start(), calls=%async_computation.4 | async-start | bytes 294912
  153.7 79.9 %reduce-scatter.5.cloned.1.call-start = ((), (), s32[]{:S(2)}) async-start(), calls=%async_computation.3 | async-start | bytes 294912 | tf_op jit(solution)/shard_map/reduce_scatter | solution.py:133
  153.7 62.0 %copy-start.3 = (u32[256]{0:T(256)S(1)}, u32[256]{0:T(256)}, u32[]{:S(2)}) copy-start(u32[256]{0:T(256)} %constant.44) | copy-start | bytes 3076
  154.7 257.1 %all-reduce.7.cloned.1.call-start = ((), (), s32[]{:S(2)}) async-start(), calls=%async_computation.5 | async-start | bytes 5242880
Sparse Core Ops, SparseCore 0:
  152.9 62.7 all-reduce.4
  219.3 192.4 all-reduce.6
Sparse Core Ops, SparseCore 1:
  155.7 36.1 reduce-scatter.6
  194.2 35.8 reduce-scatter.4
